TPU v7x, 32 devices: a whole 2x2x4 slice. The times are simulated.
32 devices in a mesh: seq: 16 (over z, y, x), dp: 2 (over core).
Axes of the slice: x: 2, y: 2, z: 4, core: 2. Of those that a mesh axis runs over, the one named last changes fastest.
Arguments:
- inputs: bfloat16 [8, 1536, 896], P('dp', 'seq'), may hold values from -6 to 6
- lengths: int32 [8, 9], P('dp'), may hold values from 0 to 1536, as said below
- w_qkv: bfloat16 [896, 1152], replicated, may hold values from -0.1875 to 0.1875
- b_qkv: bfloat16 [1152], replicated, may hold values from -3 to 3
- g_attn: bfloat16 [896], replicated, may hold values from 0.25 to 1.75
- w_out: bfloat16 [896, 896], replicated, may hold values from -1.5 to 1.5
- g_mlp: bfloat16 [896], replicated, may hold values from 0.25 to 1.75
- w_gate_up: bfloat16 [896, 9728], replicated, may hold values from -0.1875 to 0.1875
- w_down: bfloat16 [4864, 896], replicated, may hold values from -0.078125 to 0.078125
- cotangent: bfloat16 [8, 1536, 896], P('dp', 'seq'), may hold values from -6 to 6
Outputs:
- output: bfloat16 [8, 1536, 896], P('dp', 'seq')
- grad_input: float32 [8, 1536, 896], P('dp', 'seq')
- grad_qkv: float32 [896, 1152], P('seq')
- grad_bias_qkv: float32 [1152], replicated
- grad_norm_attn: float32 [896], replicated
- grad_out: float32 [896, 896], P('seq')
- grad_norm_mlp: float32 [896], replicated
- grad_gate_up: float32 [896, 9728], P('seq')
- grad_down: float32 [4864, 896], P('seq')
Inputs may be any that keep to these rules, and one draw needn't show every extreme that they name: Each row lists the lengths of the documents packed one after another from the start of a stream; nonzero entries come first, and the tokens after their sum, fewer than 96, are padding. In every group of 4 consecutive rows one row is a single document of 1536 tokens; any other document has at most 4096 tokens.
All inputs are finite; a program needn't handle non-finite values.
Results may differ from a plain program's by a relative error of at most 0.014.
Values may be sent and summed in bfloat16 or wider, within the bound.
No kernel may reach another device: no remote copies, remote signals or barrier semaphores. Data moves between devices by JAX's collectives and lax.ppermute only.
A program may use at most 576 MiB of HBM per device.

v0:
```python
import jax
import jax.numpy as jnp
from jax import lax
from jax.sharding import PartitionSpec as P

HEADS = 14
KVH = 2
HD = 64
FF = 4864
epsilon = 1e-06
rope_base = 1000000.0


def cut_along(shard, dim, devices):
    before, after = (shard.shape[:dim], shard.shape[dim + 1 :])
    return jnp.moveaxis(shard.reshape(*before, devices, -1, *after), dim, 0)


def summed_on_arrival(shard, axis, dim):
    devices = lax.axis_size(axis)
    blocks = lax.all_to_all(cut_along(shard, dim, devices), axis, 0, 0, tiled=True)
    return jnp.sum(blocks.astype(jnp.float32), axis=0)


def layout(lengths, offset, row_count):
    places = offset + jnp.arange(row_count, dtype=jnp.int32)
    ends = jnp.cumsum(lengths, axis=-1, dtype=jnp.int32)
    after = (places[None, :, None] >= ends[:, None, :]).astype(jnp.int32)
    segment = jnp.sum(after, axis=-1, dtype=jnp.int32)
    begins = jnp.sum(after * lengths[:, None, :], axis=-1, dtype=jnp.int32)
    return (segment, places[None, :] - begins, places[None, :] < ends[:, -1:])


def tables(position, head_size):
    half = head_size // 2
    inverse = rope_base ** (-(jnp.arange(half, dtype=jnp.float32) * (2.0 / head_size)))
    angle = position.astype(jnp.float32)[..., None] * inverse
    return (jnp.cos(angle)[..., None, :], jnp.sin(angle)[..., None, :])


def rotate(field, cos_table, sin_table):
    half = field.shape[-1] // 2
    first = field[..., :half]
    second = field[..., half:]
    return jnp.concatenate(
        [first * cos_table - second * sin_table, second * cos_table + first * sin_table], axis=-1
    )


def unrotate(grad_field, cos_table, sin_table):
    half = grad_field.shape[-1] // 2
    first = grad_field[..., :half]
    second = grad_field[..., half:]
    return jnp.concatenate(
        [first * cos_table + second * sin_table, second * cos_table - first * sin_table], axis=-1
    )


def transposed_product(left, right):
    return lax.dot_general(
        left, right, (((1,), (1,)), ((), ())), preferred_element_type=jnp.float32
    )


def shards(inputs, lengths, w_qkv, b_qkv, g_attn, w_out, g_mlp, w_gate_up, w_down, cotangent):
    streams, length, model_width = inputs.shape
    tokens = streams * length
    stream_len = length * lax.axis_size("seq")
    offset = lax.axis_index("seq") * length
    q_width = HEADS * HD
    kv_width = KVH * HD
    group_size = HEADS // KVH
    factor = HD ** (-0.5)
    blocks = max(1, min(16, stream_len // 512))
    key_block = stream_len // blocks
    q_seg, q_pos, valid_rows = layout(lengths, offset, length)
    k_seg, unused_pos, unused_valid = layout(lengths, 0, stream_len)
    q_place = offset + jnp.arange(length, dtype=jnp.int32)
    residual = inputs.reshape(tokens, model_width).astype(jnp.float32)
    inv_attn = lax.rsqrt(jnp.mean(residual * residual, axis=-1, keepdims=True) + epsilon)
    unit_attn = residual * inv_attn
    gain_attn = g_attn.astype(jnp.float32)
    normed = (unit_attn * gain_attn).astype(jnp.bfloat16)
    projected = jnp.dot(normed, w_qkv, preferred_element_type=jnp.float32) + b_qkv.astype(
        jnp.float32
    )
    cos_table, sin_table = tables(q_pos.reshape(tokens), HD)
    q_rot = rotate(projected[:, :q_width].reshape(tokens, HEADS, HD), cos_table, sin_table)
    k_rot = rotate(
        projected[:, q_width : q_width + kv_width].reshape(tokens, KVH, HD), cos_table, sin_table
    )
    queries = q_rot.astype(jnp.bfloat16).reshape(streams, length, KVH, group_size, HD)
    key_low = k_rot.astype(jnp.bfloat16).reshape(streams, length, kv_width)
    value_low = (
        projected[:, q_width + kv_width :].astype(jnp.bfloat16).reshape(streams, length, kv_width)
    )
    key_all, value_all = (
        lax.all_gather(key_low, "seq", axis=1, tiled=True),
        lax.all_gather(value_low, "seq", axis=1, tiled=True),
    )
    key_all = key_all.reshape(streams, stream_len, KVH, HD)
    value_all = value_all.reshape(streams, stream_len, KVH, HD)

    def scored(key_part, key_seg, first_key, rows):
        scores = (
            jnp.einsum("bqhgd,bkhd->bhgqk", queries, key_part, preferred_element_type=jnp.float32)
            * factor
        )
        key_place = first_key + jnp.arange(rows, dtype=jnp.int32)
        allowed = (q_seg[:, :, None] == key_seg[:, None, :]) & (
            q_place[None, :, None] >= key_place[None, None, :]
        )
        return (scores, allowed[:, None, None])

    def touches(first_key, rows):
        last_seg = lax.dynamic_slice_in_dim(k_seg, first_key + rows - 1, 1, 1)[:, 0]
        return jnp.any((first_key <= q_place[length - 1]) & (last_seg >= q_seg[:, 0]))

    def slices(first_key, rows, key_src, value_src):
        return (
            lax.dynamic_slice_in_dim(key_src, first_key, rows, 1),
            lax.dynamic_slice_in_dim(value_src, first_key, rows, 1),
            lax.dynamic_slice_in_dim(k_seg, first_key, rows, 1),
        )

    def softmax_stats(block_index, running):
        first_key = block_index * key_block

        def softmax_compute(state):
            row_max, row_sum = state
            key_part, unused_value, key_seg = slices(first_key, key_block, key_all, value_all)
            scores, allowed = scored(key_part, key_seg, first_key, key_block)
            masked = jnp.where(allowed, scores, -1e30)
            new_max = jnp.maximum(row_max, jnp.max(masked, axis=-1, keepdims=True))
            fresh = jnp.where(allowed, jnp.exp(masked - new_max), 0.0)
            return (
                new_max,
                row_sum * jnp.exp(row_max - new_max) + jnp.sum(fresh, axis=-1, keepdims=True),
            )

        return lax.cond(
            touches(first_key, key_block), softmax_compute, lambda state: state, running
        )

    stat_shape = (streams, KVH, group_size, length, 1)
    row_max, row_sum = lax.fori_loop(
        0,
        blocks,
        softmax_stats,
        (jnp.full(stat_shape, -1e30, jnp.float32), jnp.zeros(stat_shape, jnp.float32)),
    )
    log_sum = row_max + jnp.log(row_sum)

    def weighted(block_index, running):
        first_key = block_index * key_block

        def weighted_compute(partial_value):
            key_part, value_part, key_seg = slices(first_key, key_block, key_all, value_all)
            scores, allowed = scored(key_part, key_seg, first_key, key_block)
            weights = jnp.where(allowed, jnp.exp(scores - log_sum), 0.0).astype(jnp.bfloat16)
            return partial_value + jnp.einsum(
                "bhgqk,bkhd->bqhgd", weights, value_part, preferred_element_type=jnp.float32
            )

        return lax.cond(
            touches(first_key, key_block),
            weighted_compute,
            lambda partial_value: partial_value,
            running,
        )

    mixed_out = lax.fori_loop(
        0, blocks, weighted, jnp.zeros((streams, length, KVH, group_size, HD), jnp.float32)
    )
    mixed_low = mixed_out.reshape(tokens, q_width).astype(jnp.bfloat16)
    middle = residual + jnp.dot(mixed_low, w_out, preferred_element_type=jnp.float32)
    inv_mlp = lax.rsqrt(jnp.mean(middle * middle, axis=-1, keepdims=True) + epsilon)
    unit_mlp = middle * inv_mlp
    gain_mlp = g_mlp.astype(jnp.float32)
    normed_mlp = (unit_mlp * gain_mlp).astype(jnp.bfloat16)
    gate_up = jnp.dot(normed_mlp, w_gate_up, preferred_element_type=jnp.float32)
    gate_pre = gate_up[:, :FF]
    up_pre = gate_up[:, FF:]
    gate_sigmoid = jax.nn.sigmoid(gate_pre)
    gate_silu = jax.nn.silu(gate_pre)
    active = (gate_silu * up_pre).astype(jnp.bfloat16)
    output = (middle + jnp.dot(active, w_down, preferred_element_type=jnp.float32)).astype(
        jnp.bfloat16
    )
    seed_grad = (cotangent * valid_rows[..., None].astype(jnp.bfloat16)).reshape(
        tokens, model_width
    )
    grad_active = transposed_product(seed_grad, w_down)
    grad_gate = grad_active * up_pre * (gate_sigmoid * (1.0 + gate_pre * (1.0 - gate_sigmoid)))
    grad_up = grad_active * gate_silu
    grad_gate_up = jnp.concatenate([grad_gate, grad_up], axis=1).astype(jnp.bfloat16)
    grad_normed_mlp = transposed_product(grad_gate_up, w_gate_up)
    scaled_mlp = grad_normed_mlp * gain_mlp
    grad_middle = seed_grad.astype(jnp.float32) + inv_mlp * (
        scaled_mlp - unit_mlp * jnp.mean(scaled_mlp * unit_mlp, axis=-1, keepdims=True)
    )
    gain_mlp_part = jnp.sum(grad_normed_mlp * unit_mlp, axis=0)
    grad_branch = grad_middle.astype(jnp.bfloat16)
    grad_mixed = (
        transposed_product(grad_branch, w_out)
        .astype(jnp.bfloat16)
        .reshape(streams, length, KVH, group_size, HD)
    )
    row_delta = jnp.sum(grad_mixed.astype(jnp.float32) * mixed_out, axis=-1).transpose(0, 2, 3, 1)[
        ..., None
    ]
    key_back, value_back = (
        lax.all_gather(key_low, "seq", axis=1, tiled=True),
        lax.all_gather(value_low, "seq", axis=1, tiled=True),
    )
    key_back = key_back.reshape(streams, stream_len, KVH, HD)
    value_back = value_back.reshape(streams, stream_len, KVH, HD)

    def back_block(block_index, running):
        first_key = block_index * key_block

        def back_compute(state):
            query_grads, key_terms_all = state
            key_part, value_part, key_seg = slices(first_key, key_block, key_back, value_back)
            scores, allowed = scored(key_part, key_seg, first_key, key_block)
            weights = jnp.where(allowed, jnp.exp(scores - log_sum), 0.0)
            grad_weights = jnp.einsum(
                "bqhgd,bkhd->bhgqk", grad_mixed, value_part, preferred_element_type=jnp.float32
            )
            grad_scores = (weights * (grad_weights - row_delta)).astype(jnp.bfloat16)
            query_grads = (
                query_grads
                + jnp.einsum(
                    "bhgqk,bkhd->bqhgd", grad_scores, key_part, preferred_element_type=jnp.float32
                )
                * factor
            )
            grad_keys = (
                jnp.einsum(
                    "bhgqk,bqhgd->kbhd", grad_scores, queries, preferred_element_type=jnp.float32
                )
                * factor
            )
            grad_values = jnp.einsum(
                "bhgqk,bqhgd->kbhd",
                weights.astype(jnp.bfloat16),
                grad_mixed,
                preferred_element_type=jnp.float32,
            )
            piece = jnp.concatenate(
                [
                    grad_keys.reshape(key_block, streams, kv_width),
                    grad_values.reshape(key_block, streams, kv_width),
                ],
                axis=-1,
            )
            key_terms_all = lax.dynamic_update_slice_in_dim(key_terms_all, piece, first_key, 0)
            return (query_grads, key_terms_all)

        return lax.cond(touches(first_key, key_block), back_compute, lambda state: state, running)

    grad_queries, key_terms_all = lax.fori_loop(
        0,
        blocks,
        back_block,
        (
            jnp.zeros((streams, length, KVH, group_size, HD), jnp.float32),
            jnp.zeros((stream_len, streams, 2 * kv_width), jnp.float32),
        ),
    )
    key_grads = summed_on_arrival(key_terms_all.astype(jnp.bfloat16), "seq", 0)
    key_grads = key_grads.transpose(1, 0, 2).reshape(tokens, 2 * kv_width)
    grad_q_lin = unrotate(grad_queries.reshape(tokens, HEADS, HD), cos_table, sin_table).reshape(
        tokens, q_width
    )
    grad_k_lin = unrotate(
        key_grads[:, :kv_width].reshape(tokens, KVH, HD), cos_table, sin_table
    ).reshape(tokens, kv_width)
    grad_projected = jnp.concatenate(
        [grad_q_lin, grad_k_lin, key_grads[:, kv_width:]], axis=1
    ).astype(jnp.bfloat16)
    grad_normed = transposed_product(grad_projected, w_qkv)
    scaled_attn = grad_normed * gain_attn
    grad_input = grad_middle + inv_attn * (
        scaled_attn - unit_attn * jnp.mean(scaled_attn * unit_attn, axis=-1, keepdims=True)
    )
    gain_attn_part = jnp.sum(grad_normed * unit_attn, axis=0)
    bias_part = jnp.sum(grad_projected.astype(jnp.float32), axis=0)

    def make_rows():

        def product(left, right):
            return lax.dot_general(
                left, right, (((0,), (0,)), ((), ())), preferred_element_type=jnp.float32
            )

        def row_terms(first_col, col_count):
            return jnp.concatenate(
                [
                    product(normed, grad_projected),
                    product(mixed_low, grad_branch),
                    product(normed_mlp, grad_gate_up),
                ],
                axis=1,
            )

        def down_terms(first_col, col_count):
            return product(active, seed_grad)

        return (row_terms, down_terms)

    row_share = model_width // lax.axis_size("seq")
    hidden_share = FF // lax.axis_size("seq")
    row_terms, down_terms = make_rows()
    row_part = lax.psum_scatter(
        row_terms(jnp.int32(0), row_share * lax.axis_size("seq")),
        "seq",
        scatter_dimension=0,
        tiled=True,
    )
    down_part = summed_on_arrival(
        down_terms(jnp.int32(0), hidden_share * lax.axis_size("seq")).astype(jnp.bfloat16), "seq", 0
    )
    row_part, down_part = (
        lax.psum(row_part.astype(jnp.bfloat16), "dp").astype(jnp.float32),
        lax.psum(down_part.astype(jnp.bfloat16), "dp").astype(jnp.float32),
    )
    bias_grad, gain_attn_grad, gain_mlp_grad = lax.psum(
        (bias_part, gain_attn_part, gain_mlp_part), ("seq", "dp")
    )
    joined_width = q_width + 2 * kv_width
    return (
        output.reshape(streams, length, model_width),
        grad_input.reshape(streams, length, model_width),
        row_part[:, :joined_width],
        bias_grad,
        gain_attn_grad,
        row_part[:, joined_width : joined_width + model_width],
        gain_mlp_grad,
        row_part[:, joined_width + model_width :],
        down_part,
    )


def solution(mesh):
    in_specs = (
        P("dp", "seq", None),
        P("dp", None),
        P(),
        P(),
        P(),
        P(),
        P(),
        P(),
        P(),
        P("dp", "seq", None),
    )
    out_specs = (
        P("dp", "seq", None),
        P("dp", "seq", None),
        P("seq", None),
        P(),
        P(),
        P("seq", None),
        P(),
        P("seq", None),
        P("seq", None),
    )
    return jax.shard_map(shards, mesh=mesh, in_specs=in_specs, out_specs=out_specs, check_vma=False)
```

profile of v0, /device:TPU:6, one launch (start us, length us, event | category | flops | bytes accessed | tf_op | source)
XLA Modules:
  0.0 1464.1 jit_solution(16891637317464104812)
XLA Ops:
  19.0 2.5 slice.163
  29.2 46.4 %all-gather.5.cloned.1.call-done = bf16[4,1536,128]{2,0,1:T(4,128)(2,1)} async-done(((bf16[4,96,128]{2,0,1:T(4,128)(2,1)}), bf16[4,1536,128]{2,0,1:T(4,128)(2,1)}) %all-gather.5.cloned.1.call-update) | async-done | bytes 1572880 | tf_op jit(solution)/shard_map/all_gather | solution.py:98
  75.6 3.9 copy.106
  79.5 15.1 %while.58 = (s32[]{:T(128)}, f32[4,2,7,96,1]{3,2,1,0,4:T(8,128)S(1)}, f32[4,2,7,96,1]{3,2,1,0,4:T(8,128)S(1)}, s32[96]{0:T(128)S(1)}, s32[4,1536]{1,0:T(4,128)S(...) while((s32[]{:T(128)}, ...), condition=%wide.region_11.12_spmd, body=%wide.region_5.11_spmd.sunk | while | flops 374795296 | bytes 24231176 | solution.py:146
  82.1 7.2 conditional.6
  82.5 3.3 fusion
  85.8 3.5 select_reduce_fusion
  94.6 40.9 %all-gather.3.cloned.1.call-done = bf16[4,1536,128]{2,1,0:T(8,128)(2,1)} async-done(((bf16[4,96,128]{2,1,0:T(8,128)(2,1)}), bf16[4,1536,128]{2,1,0:T(8,128)(2,1)}) %all-gather.3.cloned.1.call-update) | async-done | bytes 1572880 | tf_op jit(solution)/shard_map/all_gather | solution.py:99
  135.5 2.6 copy.102
  139.5 15.9 %while.59 = (s32[]{:T(128)}, f32[4,96,2,7,64]{1,4,3,2,0:T(8,128)}, s32[96]{0:T(128)S(1)}, s32[4,1536]{1,0:T(4,128)S(1)}, s32[4,96]{1,0:T(4,128)S(1)}, /*index=5*...) while((s32[]{:T(128)}, f32[4,96,2,7,64]{1,4,3,2,0:T(8,128)}, ...), condition=%wide.region_16.17_spmd, body=%wide.region_12.16_spmd.sunk | while | flops 716440064 | bytes 5492981 | solution.py:172
  142.1 8.1 conditional.7
  142.5 7.7 bitcast_add_fusion.1
  158.8 2.6 convert_element_type.165
  161.4 2.9 multiply_reduce_fusion.4
  164.3 17.4 %fusion.57 = f32[384,9728]{1,0:T(8,128)} fusion(bf16[896,9728]{1,0:T(8,128)(2,1)} %param.29, f32[384,896]{1,0:T(8,128)S(1)} %get-tuple-element.1328, f32[896]{0:T(1024)S(1)} %convert_element_type.166, f32[384]{0:T(512)S(1)} %add_rsqrt_fusion), kind=kOutput, calls=%fused_computation.134 | convolution fusion | flops 6695141376 | bytes 33756160 | tf_op jit(solution)/shard_map/dot_general | solution.py:181
  181.7 14.5 multiply_convert_fusion.1
  196.2 16.0 %multiply_reduce_fusion = (f32[896]{0:T(1024)}, f32[384]{0:T(512)S(1)}, f32[384,896]{1,0:T(8,128)}) fusion(f32[384,896]{1,0:T(8,128)} %copy-done.8, f32[384]{0:T(512)S(1)} %add_rsqrt_fusion, f32[896]{0:T(1024)S(1)} %convert_element_type.166, bf16[896,9728]{1,0:T(8,128)(2,1)} %param.29, bf16[384,4864]{1,0:T(8,128)(2,1)} %get-tuple-element.1315, ...), kind=kOutput, calls=%fused_computation.84 | convolution fusion | flops 6711114240 | bytes 27666432 | tf_op jit(solution)/shard_map/dot_general | solution.py:60
  212.2 2.4 multiply_add_fusion.1
  217.7 2.2 copy.111
  219.9 3.4 reshape.367
  223.3 3.3 fusion.49
  231.2 25.8 %while.60 = (s32[]{:T(128)}, f32[4,96,2,7,64]{1,4,3,2,0:T(8,128)}, bf16[1536,4,256]{0,2,1:T(8,128)(2,1)}, s32[96]{0:T(128)S(1)}, s32[4,1536]{1,0:T(4,128)S(1)}, ...) while((s32[]{:T(128)}, f32[4,96,2,7,64]{1,4,3,2,0:T(8,128)}, ...), condition=%wide.region_24.25_spmd, body=%wide.region_20.24_spmd.sunk | while | flops 1792885248 | bytes 74315176 | solution.py:262
  233.8 18.0 %conditional.8 = ((f32[4,96,2,7,64]{1,4,3,2,0:T(8,128)}, bf16[1536,4,256]{0,2,1:T(8,128)(2,1)})) conditional(s32[]{:T(128)} %convert_element_type.222, (f32[4,96,2,7,64]{1,4,3,2,0:T(8,128)}, bf16[1536,4,256]{0,2,1:T(8,128)(2,1)}) %tuple.195, (s32[]{:T(128)}, bf16[4,1536,2,64]{1,3,2,0:T(8,128)(2,1)}, s32[4,96]{1,0:T(4,128)S(1)}, ...), branch_computations={%region_22.22_spmd, %region_23.23_spmd} | conditional | flops 1792885248 | bytes 74314792 | solution.py:260
  234.2 2.7 fusion.36
  236.9 2.9 fusion.30
  239.8 5.0 fusion.26
  246.4 3.1 bitcast_add_fusion.2
  257.0 4.7 copy.117
  261.7 3.8 copy.118
  265.6 57.8 %all-to-all-start = ((bf16[16,96,4,256]{3,1,2,0:T(8,128)(2,1)}), bf16[16,96,4,256]{3,1,2,0:T(8,128)(2,1)}, u32[]{:S(2)}, u32[]{:S(2)}) async-start(bf16[16,96,4,256]{3,1,2,0:T(8,128)(2,1)} %copy.118), calls=%async_computation | async-start | bytes 6291456 | tf_op jit(solution)/shard_map/all_to_all | solution.py:21
  323.4 3.9 copy.116
  327.3 3.1 reshape.368
  333.1 2.7 fusion.50
  335.8 18.5 %fusion.47 = f32[896,9728]{1,0:T(8,128)} fusion(bf16[384,4864]{1,0:T(8,128)(2,1)} %get-tuple-element.1315, bf16[384,4864]{1,0:T(8,128)(2,1)} %get-tuple-element.1314, f32[384,896]{1,0:T(8,128)} %copy-done.8, f32[896]{0:T(1024)S(1)} %convert_element_type.166, f32[384]{0:T(512)S(1)} %add_rsqrt_fusion), kind=kOutput, calls=%fused_computation.76 | convolution fusion | flops 6710083584 | bytes 43717632 | tf_op jit(solution)/shard_map/dot_general | solution.py:293
  354.3 31.3 %all-to-all-done = bf16[16,96,4,256]{3,1,2,0:T(8,128)(2,1)} async-done(((bf16[16,96,4,256]{3,1,2,0:T(8,128)(2,1)}), bf16[16,96,4,256]{3,1,2,0:T(8,128)(2,1)}, u32[]{:S(2)}, u32[]{:S(2)}) %all-to-all-start) | async-done | bytes 3145760 | tf_op jit(solution)/shard_map/all_to_all | solution.py:21
  385.6 2.5 convert_reduce_fusion
  393.8 4.8 fusion.58
  398.6 29.1 %pad_maximum_fusion = f32[896,11776]{1,0:T(8,128)} fusion(f32[896,9728]{1,0:T(8,128)} %fusion.47, f32[896,896]{1,0:T(8,128)} %fusion.50, f32[896,1152]{1,0:T(8,128)} %fusion.58), kind=kLoop, calls=%fused_computation.67 | loop fusion | flops 21102592 | bytes 84410368 | tf_op jit(solution)/shard_map/concatenate | solution.py:298
  427.8 7.2 convolution_convert_fusion
  435.0 292.5 %all_to_all.10 = bf16[16,304,896]{2,1,0:T(8,128)(2,1)} all-to-all(bf16[16,304,896]{2,1,0:T(8,128)(2,1)S(1)} %bitcast.171), channel_id=1, replica_groups=mesh['seq'=16,'dp'=2] {'seq'}, dimensions={0} | all-to-all | bytes 17432576 | tf_op jit(solution)/shard_map/all_to_all | solution.py:21
  727.4 5.8 reduce_sum.141
  733.2 653.0 %reduce-scatter.2.cloned.1.call-done = f32[56,11776]{1,0:T(8,128)} async-done(((f32[896,11776]{1,0:T(8,128)}), f32[56,11776]{1,0:T(8,128)}) %reduce-scatter.2.cloned.1.call-update) | async-done | bytes 2637840 | tf_op jit(solution)/shard_map/reduce_scatter | solution.py:315
  1386.3 2.9 convert_element_type.177
  1389.3 9.9 add_convert_fusion
  1399.4 3.0 multiply_reduce_fusion.1
  1402.4 44.2 %all-reduce = (f32[1152]{0:T(1024)}, f32[896]{0:T(1024)}, f32[896]{0:T(1024)}) all-reduce(f32[1152]{0:T(1024)S(1)} %convert_reduce_fusion.1, f32[896]{0:T(1024)} %get-tuple-element.1245, f32[896]{0:T(1024)} %get-tuple-element.1243), channel_id=1, replica_groups=mesh['seq'=16,'dp'=2] {'seq','dp'}, use_global_device_ids=true, to_apply=%region_30.31 | all-reduce | flops 2944 | bytes 23552 | tf_op jit(solution)/shard_map/psum | solution.py:328
  1447.3 3.0 multiply_add_fusion
  1453.5 2.8 slice.176
  (168 shorter events, 61.7 us)
Async XLA Ops:
  7.2 6.3 copy-start
  7.2 68.4 %all-gather.5.cloned.1.call-start = ((), (), s32[]{:S(2)}) async-start(), calls=%async_computation.4 | async-start | bytes 1671168 | tf_op jit(solution)/shard_map/all_gather | solution.py:98
  10.4 4.2 copy-start.25
  11.1 3.5 copy-start.23
  11.2 3.4 copy-start.21
  13.5 1.2 copy-start.9
  14.7 1.2 copy-start.12
  16.0 5.4 copy-start.27
  16.3 6.9 copy-start.13
  16.3 6.9 copy-start.15
  17.3 118.2 %all-gather.3.cloned.1.call-start = ((), (), s32[]{:S(2)}) async-start(), calls=%async_computation.3 | async-start | bytes 1671168 | tf_op jit(solution)/shard_map/all_gather | solution.py:99
  25.6 2.4 copy-start.22
  26.8 1.4 copy-start.19
  164.2 17.5 %copy-start.8 = (f32[384,896]{1,0:T(8,128)}, f32[384,896]{1,0:T(8,128)S(1)}, u32[]{:S(2)}) copy-start(f32[384,896]{1,0:T(8,128)S(1)} %get-tuple-element.1328) | copy-start | bytes 4128772
  164.3 17.4 %copy-start.10 = (bf16[4,96,896]{2,1,0:T(8,128)(2,1)S(1)}, bf16[4,96,896]{2,1,0:T(8,128)(2,1)}, u32[]{:S(2)}) copy-start(bf16[4,96,896]{2,1,0:T(8,128)(2,1)} %broadcast_multiply_fusion) | copy-start | bytes 2064388
  212.2 3.6 copy-start.28
  214.7 1.2 copy-start.3
  223.3 3.4 copy-start.5
  234.2 2.8 copy-start.17
  244.9 1.5 copy-start.1
  249.5 1.2 copy-start.2
  265.6 120.0 %all-to-all-start = ((bf16[16,96,4,256]{3,1,2,0:T(8,128)(2,1)}), bf16[16,96,4,256]{3,1,2,0:T(8,128)(2,1)}, u32[]{:S(2)}, u32[]{:S(2)}) async-start(bf16[16,96,4,256]{3,1,2,0:T(8,128)(2,1)} %copy.118), calls=%async_computation | async-start | bytes 6291456 | tf_op jit(solution)/shard_map/all_to_all | solution.py:21
  323.3 1063.0 %reduce-scatter.2.cloned.1.call-start = ((), (), s32[]{:S(2)}) async-start(), calls=%async_computation.5 | async-start | bytes 44843008 | tf_op jit(solution)/shard_map/reduce_scatter | solution.py:315
  327.3 3.1 copy-start.14
  327.3 3.1 copy-start.16
  330.4 2.6 copy-start.4
  330.4 2.6 copy-start.11
  427.7 1022.6 %all-reduce.4.cloned.1.call-start = ((), (), s32[]{:S(2)}) async-start(), calls=%async_computation.6 | async-start | bytes 3727360 | tf_op jit(solution)/shard_map/psum | solution.py:325
  1389.2 9.9 copy-start.7
  1389.2 9.9 copy-start.18
  1389.3 10.2 copy-start.6
  1389.3 10.2 copy-start.24
  1389.3 10.1 copy-start.26
  1453.5 2.8 copy-start.20
Sparse Core Ops, SparseCore 0:
  17.4 58.1 all-gather.4
  78.8 56.6 all-gather.2
  427.9 958.3 reduce-scatter.1
  1389.4 22.3 all-reduce.3
where the time goes:
time: 1470 us; the launch traced here: 1460 us
  waiting for transfers between devices  772 us (53%)
  blocking collectives  337 us (23%)
  matrix products  126 us (9%)
  other arithmetic  76.5 us (5%)
  local copies, waits for them, and re-layouts  68.9 us (5%)
  starting transfers between devices  57.9 us (4%)
    reduce_scatter x1, waiting for transfers between devices, shards(): lax.psum_scatter(row_terms(jnp.int32(0), row_share * lax.axis_size('seq')...  653 us
    all_to_all x1, blocking collectives, summed_on_arrival(): lax.all_to_all(cut_along(shard, dim, devices), axis, 0, 0, tiled=True)  292 us
    all_to_all x1, starting transfers between devices, summed_on_arrival(): lax.all_to_all(cut_along(shard, dim, devices), axis, 0, 0, tiled=True)  57.8 us
    all_gather x1, waiting for transfers between devices, shards(): lax.all_gather(key_low, 'seq', axis=1, tiled=True)  46.4 us
    psum x1, blocking collectives, shards(): lax.psum((bias_part, gain_attn_part, gain_mlp_part), ('seq', 'dp'))  44.2 us
    all_gather x1, waiting for transfers between devices, shards(): lax.all_gather(value_low, 'seq', axis=1, tiled=True)  40.9 us
    dot_general x4, matrix products, transposed_product(): lax.dot_general(left, right, (((1,), (1,)), ((), ())), preferred_element_...  35.4 us
    dot_general x4, matrix products, product(): lax.dot_general(left, right, (((0,), (0,)), ((), ())), preferred_element_...  33.2 us
  transfers between devices with their start and end apart: 5, of which 4 were waited for; matrix products, arithmetic and copies ran while one was open for 6% of the time, Pallas kernels for 0%

commit v1 on v0

--- a/solution.py
+++ b/solution.py
@@ -96,7 +96,9 @@
     )
     key_all, value_all = (
         lax.all_gather(key_low, "seq", axis=1, tiled=True),
-        lax.all_gather(value_low, "seq", axis=1, tiled=True),
+        jnp.concatenate(
+            lax.all_to_all(jnp.stack([value_low] * lax.axis_size("seq")), "seq", 0, 0), axis=1
+        ),
     )
     key_all = key_all.reshape(streams, stream_len, KVH, HD)
     value_all = value_all.reshape(streams, stream_len, KVH, HD)

time: 1470 us -> 1470 us (level)
  waiting for transfers between devices: 772 us -> 736 us
  starting transfers between devices: 57.9 us -> 79.4 us
    all_gather x1, waiting for transfers between devices: 40.9 us -> 0.02 us  [shards(): lax.all_gather(value_low, 'seq', axis=1, tiled=True)]
  transfers between devices with their start and end apart: 5 -> 6, of which waited for: 4 -> 3; matrix products, arithmetic and copies ran while one was open for 6% -> 13% of each run, Pallas kernels for 0% -> 0%
where the time goes in v1:
time: 1470 us; the launch traced here: 1460 us
  waiting for transfers between devices  736 us (50%)
  blocking collectives  337 us (23%)
  matrix products  126 us (9%)
  local copies, waits for them, and re-layouts  80.4 us (5%)
  starting transfers between devices  79.4 us (5%)
  other arithmetic  75.9 us (5%)
    reduce_scatter x1, waiting for transfers between devices, shards(): lax.psum_scatter(row_terms(jnp.int32(0), row_share * lax.axis_size('seq')...  653 us
    all_to_all x1, blocking collectives, summed_on_arrival(): lax.all_to_all(cut_along(shard, dim, devices), axis, 0, 0, tiled=True)  293 us
    all_to_all x1, starting transfers between devices, summed_on_arrival(): lax.all_to_all(cut_along(shard, dim, devices), axis, 0, 0, tiled=True)  72 us
    all_gather x1, waiting for transfers between devices, shards(): lax.all_gather(key_low, 'seq', axis=1, tiled=True)  50.6 us
    psum x1, blocking collectives, shards(): lax.psum((bias_part, gain_attn_part, gain_mlp_part), ('seq', 'dp'))  44.2 us
    dot_general x4, matrix products, transposed_product(): lax.dot_general(left, right, (((1,), (1,)), ((), ())), preferred_element_...  35.4 us
    dot_general x4, matrix products, product(): lax.dot_general(left, right, (((0,), (0,)), ((), ())), preferred_element_...  33.4 us
    all_to_all x1, waiting for transfers between devices, summed_on_arrival(): lax.all_to_all(cut_along(shard, dim, devices), axis, 0, 0, tiled=True)  31.3 us
  transfers between devices with their start and end apart: 6, of which 3 were waited for; matrix products, arithmetic and copies ran while one was open for 13% of the time, Pallas kernels for 0%

profile of v1, /device:TPU:6, one launch (start us, length us, event | category | flops | bytes accessed | tf_op | source)
XLA Modules:
  0.0 1460.8 jit_solution(10166533767930600797)
XLA Ops:
  19.7 7.3 all-to-all-start
  27.7 2.5 slice.163
  38.0 50.6 %all-gather.3.cloned.1.call-done = bf16[4,1536,128]{2,0,1:T(4,128)(2,1)} async-done(((bf16[4,96,128]{2,0,1:T(4,128)(2,1)}), bf16[4,1536,128]{2,0,1:T(4,128)(2,1)}) %all-gather.3.cloned.1.call-update) | async-done | bytes 1572880 | tf_op jit(solution)/shard_map/all_gather | solution.py:98
  88.6 3.9 copy.111
  92.5 15.1 %while.58 = (s32[]{:T(128)}, f32[4,2,7,96,1]{3,2,1,0,4:T(8,128)S(1)}, f32[4,2,7,96,1]{3,2,1,0,4:T(8,128)S(1)}, s32[96]{0:T(128)S(1)}, s32[4,1536]{1,0:T(4,128)S(...) while((s32[]{:T(128)}, ...), condition=%wide.region_11.12_spmd, body=%wide.region_5.11_spmd.sunk | while | flops 374795296 | bytes 24231176 | solution.py:148
  95.1 7.2 conditional.6
  95.5 3.3 fusion
  98.8 3.5 select_reduce_fusion
  107.6 4.4 copy.107
  112.0 4.6 reshape_reshape.3
  118.1 15.9 %while.59 = (s32[]{:T(128)}, f32[4,96,2,7,64]{1,4,3,2,0:T(8,128)}, s32[96]{0:T(128)S(1)}, s32[4,1536]{1,0:T(4,128)S(1)}, s32[4,96]{1,0:T(4,128)S(1)}, /*index=5*...) while((s32[]{:T(128)}, f32[4,96,2,7,64]{1,4,3,2,0:T(8,128)}, ...), condition=%wide.region_16.17_spmd, body=%wide.region_12.16_spmd.sunk | while | flops 716440064 | bytes 5492981 | solution.py:174
  120.7 8.1 conditional.7
  121.1 7.7 bitcast_add_fusion.1
  137.4 3.0 convert_element_type.165
  140.3 2.9 multiply_reduce_fusion.4
  143.3 17.3 %fusion.57 = f32[384,9728]{1,0:T(8,128)} fusion(bf16[896,9728]{1,0:T(8,128)(2,1)} %param.29, f32[384,896]{1,0:T(8,128)S(1)} %get-tuple-element.1328, f32[896]{0:T(1024)S(1)} %convert_element_type.166, f32[384]{0:T(512)S(1)} %add_rsqrt_fusion), kind=kOutput, calls=%fused_computation.134 | convolution fusion | flops 6695141376 | bytes 33756160 | tf_op jit(solution)/shard_map/dot_general | solution.py:183
  160.6 14.5 multiply_convert_fusion.1
  175.0 16.1 %multiply_reduce_fusion = (f32[896]{0:T(1024)}, f32[384]{0:T(512)S(1)}, f32[384,896]{1,0:T(8,128)}) fusion(f32[384,896]{1,0:T(8,128)} %copy-done.8, f32[384]{0:T(512)S(1)} %add_rsqrt_fusion, f32[896]{0:T(1024)S(1)} %convert_element_type.166, bf16[896,9728]{1,0:T(8,128)(2,1)} %param.29, bf16[384,4864]{1,0:T(8,128)(2,1)} %get-tuple-element.1315, ...), kind=kOutput, calls=%fused_computation.84 | convolution fusion | flops 6711114240 | bytes 27666432 | tf_op jit(solution)/shard_map/dot_general | solution.py:60
  198.8 3.2 reshape.369
  204.5 2.8 fusion.49
  207.4 2.6 copy.116
  213.3 25.8 %while.60 = (s32[]{:T(128)}, f32[4,96,2,7,64]{1,4,3,2,0:T(8,128)}, bf16[1536,4,256]{0,2,1:T(8,128)(2,1)}, s32[96]{0:T(128)S(1)}, s32[4,1536]{1,0:T(4,128)S(1)}, ...) while((s32[]{:T(128)}, f32[4,96,2,7,64]{1,4,3,2,0:T(8,128)}, ...), condition=%wide.region_24.25_spmd, body=%wide.region_20.24_spmd.sunk | while | flops 1792885248 | bytes 74315176 | solution.py:264
  215.9 18.0 %conditional.8 = ((f32[4,96,2,7,64]{1,4,3,2,0:T(8,128)}, bf16[1536,4,256]{0,2,1:T(8,128)(2,1)})) conditional(s32[]{:T(128)} %convert_element_type.222, (f32[4,96,2,7,64]{1,4,3,2,0:T(8,128)}, bf16[1536,4,256]{0,2,1:T(8,128)(2,1)}) %tuple.195, (s32[]{:T(128)}, bf16[4,1536,2,64]{1,3,2,0:T(8,128)(2,1)}, s32[4,96]{1,0:T(4,128)S(1)}, ...), branch_computations={%region_22.22_spmd, %region_23.23_spmd} | conditional | flops 1792885248 | bytes 74314792 | solution.py:262
  216.3 2.7 fusion.36
  219.0 2.9 fusion.30
  221.9 5.0 fusion.26
  228.5 3.1 bitcast_add_fusion.2
  239.1 4.7 copy.123
  243.8 3.8 copy.124
  247.6 72.0 %all-to-all-start.1 = ((bf16[16,96,4,256]{3,1,2,0:T(8,128)(2,1)}), bf16[16,96,4,256]{3,1,2,0:T(8,128)(2,1)}, u32[]{:S(2)}, u32[]{:S(2)}) async-start(bf16[16,96,4,256]{3,1,2,0:T(8,128)(2,1)} %copy.124), calls=%async_computation.1 | async-start | bytes 6291456 | tf_op jit(solution)/shard_map/all_to_all | solution.py:21
  319.7 3.9 copy.122
  323.6 3.2 reshape.370
  329.4 2.7 fusion.50
  332.2 18.6 %fusion.47 = f32[896,9728]{1,0:T(8,128)} fusion(bf16[384,4864]{1,0:T(8,128)(2,1)} %get-tuple-element.1315, bf16[384,4864]{1,0:T(8,128)(2,1)} %get-tuple-element.1314, f32[384,896]{1,0:T(8,128)} %copy-done.8, f32[896]{0:T(1024)S(1)} %convert_element_type.166, f32[384]{0:T(512)S(1)} %add_rsqrt_fusion), kind=kOutput, calls=%fused_computation.76 | convolution fusion | flops 6710083584 | bytes 43717632 | tf_op jit(solution)/shard_map/dot_general | solution.py:295
  350.8 31.3 %all-to-all-done.1 = bf16[16,96,4,256]{3,1,2,0:T(8,128)(2,1)} async-done(((bf16[16,96,4,256]{3,1,2,0:T(8,128)(2,1)}), bf16[16,96,4,256]{3,1,2,0:T(8,128)(2,1)}, u32[]{:S(2)}, u32[]{:S(2)}) %all-to-all-start.1) | async-done | bytes 3145760 | tf_op jit(solution)/shard_map/all_to_all | solution.py:21
  382.0 2.5 convert_reduce_fusion
  390.3 4.8 fusion.58
  395.1 29.1 %pad_maximum_fusion = f32[896,11776]{1,0:T(8,128)} fusion(f32[896,9728]{1,0:T(8,128)} %fusion.47, f32[896,896]{1,0:T(8,128)} %fusion.50, f32[896,1152]{1,0:T(8,128)} %fusion.58), kind=kLoop, calls=%fused_computation.67 | loop fusion | flops 21102592 | bytes 84410368 | tf_op jit(solution)/shard_map/concatenate | solution.py:300
  424.3 7.2 convolution_convert_fusion
  431.5 292.6 %all_to_all.15 = bf16[16,304,896]{2,1,0:T(8,128)(2,1)} all-to-all(bf16[16,304,896]{2,1,0:T(8,128)(2,1)S(1)} %bitcast.176), channel_id=1, replica_groups=mesh['seq'=16,'dp'=2] {'seq'}, dimensions={0} | all-to-all | bytes 17432576 | tf_op jit(solution)/shard_map/all_to_all | solution.py:21
  724.1 5.8 reduce_sum.141
  729.9 652.9 %reduce-scatter.2.cloned.1.call-done = f32[56,11776]{1,0:T(8,128)} async-done(((f32[896,11776]{1,0:T(8,128)}), f32[56,11776]{1,0:T(8,128)}) %reduce-scatter.2.cloned.1.call-update) | async-done | bytes 2637840 | tf_op jit(solution)/shard_map/reduce_scatter | solution.py:317
  1382.8 2.9 convert_element_type.177
  1385.8 9.9 add_convert_fusion
  1396.0 3.0 multiply_reduce_fusion.1
  1398.9 44.2 %all-reduce = (f32[1152]{0:T(1024)}, f32[896]{0:T(1024)}, f32[896]{0:T(1024)}) all-reduce(f32[1152]{0:T(1024)S(1)} %convert_reduce_fusion.1, f32[896]{0:T(1024)} %get-tuple-element.1245, f32[896]{0:T(1024)} %get-tuple-element.1243), channel_id=1, replica_groups=mesh['seq'=16,'dp'=2] {'seq','dp'}, use_global_device_ids=true, to_apply=%region_30.31 | all-reduce | flops 2944 | bytes 23552 | tf_op jit(solution)/shard_map/psum | solution.py:330
  1443.8 3.0 multiply_add_fusion
  1450.0 2.8 slice.176
  (175 shorter events, 69.3 us)
Async XLA Ops:
  7.2 6.3 copy-start
  7.2 81.4 %all-gather.3.cloned.1.call-start = ((), (), s32[]{:S(2)}) async-start(), calls=%async_computation.4 | async-start | bytes 1671168 | tf_op jit(solution)/shard_map/all_gather | solution.py:98
  10.4 4.2 copy-start.26
  11.1 3.5 copy-start.24
  11.2 3.4 copy-start.22
  13.5 1.2 copy-start.9
  14.7 1.2 copy-start.12
  16.3 15.7 %copy-start.13 = (f32[384,32]{0,1:T(8,128)}, f32[384,32]{0,1:T(8,128)S(1)}, u32[]{:S(2)}) copy-start(f32[384,32]{0,1:T(8,128)S(1)} %get-tuple-element.1325) | copy-start | bytes 147460
  16.3 15.7 %copy-start.15 = (f32[384,32]{0,1:T(8,128)}, f32[384,32]{0,1:T(8,128)S(1)}, u32[]{:S(2)}) copy-start(f32[384,32]{0,1:T(8,128)S(1)} %get-tuple-element.1326) | copy-start | bytes 147460
  18.2 1.5 copy-start.18
  19.7 87.9 %all-to-all-start = ((bf16[16,4,96,128]{3,2,1,0:T(8,128)(2,1)}), bf16[16,4,96,128]{3,2,1,0:T(8,128)(2,1)}, u32[]{:S(2)}, u32[]{:S(2)}) async-start(bf16[16,4,96,128]{3,2,1,0:T(8,128)(2,1)} %stack.3), calls=%async_computation | async-start | bytes 3145728 | tf_op jit(solution)/shard_map/all_to_all | solution.py:100
  27.0 3.3 copy-start.28
  27.0 180.4 %all-gather.5.cloned.1.call-start = ((), (), s32[]{:S(2)}) async-start(), calls=%async_computation.5 | async-start | bytes 1671168 | tf_op jit(solution)/shard_map/all_gather | solution.py:216
  34.4 2.4 copy-start.23
  35.6 1.4 copy-start.20
  143.2 17.3 %copy-start.8 = (f32[384,896]{1,0:T(8,128)}, f32[384,896]{1,0:T(8,128)S(1)}, u32[]{:S(2)}) copy-start(f32[384,896]{1,0:T(8,128)S(1)} %get-tuple-element.1328) | copy-start | bytes 4128772
  143.2 17.3 %copy-start.10 = (bf16[4,96,896]{2,1,0:T(8,128)(2,1)S(1)}, bf16[4,96,896]{2,1,0:T(8,128)(2,1)}, u32[]{:S(2)}) copy-start(bf16[4,96,896]{2,1,0:T(8,128)(2,1)} %broadcast_multiply_fusion) | copy-start | bytes 2064388
  191.1 3.6 copy-start.29
  193.6 1.2 copy-start.4
  202.0 2.5 copy-start.3
  216.3 2.8 copy-start.17
  227.0 1.5 copy-start.1
  231.6 1.2 copy-start.2
  247.6 134.4 %all-to-all-start.1 = ((bf16[16,96,4,256]{3,1,2,0:T(8,128)(2,1)}), bf16[16,96,4,256]{3,1,2,0:T(8,128)(2,1)}, u32[]{:S(2)}, u32[]{:S(2)}) async-start(bf16[16,96,4,256]{3,1,2,0:T(8,128)(2,1)} %copy.124), calls=%async_computation.1 | async-start | bytes 6291456 | tf_op jit(solution)/shard_map/all_to_all | solution.py:21
  319.6 1063.2 %reduce-scatter.2.cloned.1.call-start = ((), (), s32[]{:S(2)}) async-start(), calls=%async_computation.6 | async-start | bytes 44843008 | tf_op jit(solution)/shard_map/reduce_scatter | solution.py:317
  323.6 3.2 copy-start.14
  323.6 3.2 copy-start.16
  326.8 2.6 copy-start.5
  326.8 2.6 copy-start.11
  424.2 1022.6 %all-reduce.4.cloned.1.call-start = ((), (), s32[]{:S(2)}) async-start(), calls=%async_computation.7 | async-start | bytes 3727360 | tf_op jit(solution)/shard_map/psum | solution.py:327
  1385.8 9.9 copy-start.7
  1385.8 9.9 copy-start.19
  1385.8 10.2 copy-start.6
  1385.8 10.2 copy-start.25
  1385.8 10.2 copy-start.27
  1450.0 2.8 copy-start.21
Sparse Core Ops, SparseCore 0:
  17.4 71.0 all-gather.2
  91.8 56.6 all-gather.4
  424.3 958.4 reduce-scatter.1
  1385.9 22.2 all-reduce.3
